TPU v7x, 32 devices: a whole 2x2x4 slice. The times are simulated.
32 devices in a mesh: dp: 8 (over y, x, core), seq: 4 (over z).
Axes of the slice: x: 2, y: 2, z: 4, core: 2. Of those that a mesh axis runs over, the one named last changes fastest.
Arguments:
- tokens: bfloat16 [2, 8, 2048, 768], P(None, 'dp', 'seq'), may hold values from -6 to 6
- seq_lengths: int32 [2, 8], P(None, 'dp'), may hold values from 512 to 2048, as said below
- query_weight: bfloat16 [768, 768], P(('dp', 'seq')), may hold values from -0.21875 to 0.21875
- query_bias: bfloat16 [768], P(('dp', 'seq')), may hold values from -3 to 3
- key_weight: bfloat16 [768, 768], P(('dp', 'seq')), may hold values from -0.21875 to 0.21875
- key_bias: bfloat16 [768], P(('dp', 'seq')), may hold values from -3 to 3
- value_weight: bfloat16 [768, 768], P(('dp', 'seq')), may hold values from -0.21875 to 0.21875
- value_bias: bfloat16 [768], P(('dp', 'seq')), may hold values from -3 to 3
- output_weight: bfloat16 [768, 768], P(('dp', 'seq')), may hold values from -1.25 to 1.25
- output_bias: bfloat16 [768], P(('dp', 'seq')), may hold values from -3 to 3
- gain_first: bfloat16 [768], P(('dp', 'seq')), may hold values from 0.5 to 1.5
- shift_first: bfloat16 [768], P(('dp', 'seq')), may hold values from -3 to 3
- inner_weight: bfloat16 [768, 3072], P(('dp', 'seq')), may hold values from -0.21875 to 0.21875
- inner_bias: bfloat16 [3072], P(('dp', 'seq')), may hold values from -3 to 3
- outer_weight: bfloat16 [3072, 768], P(('dp', 'seq')), may hold values from -0.109375 to 0.109375
- outer_bias: bfloat16 [768], P(('dp', 'seq')), may hold values from -3 to 3
- gain_second: bfloat16 [768], P(('dp', 'seq')), may hold values from 0.5 to 1.5
- shift_second: bfloat16 [768], P(('dp', 'seq')), may hold values from -3 to 3
- cotangent: bfloat16 [2, 8, 2048, 768], P(None, 'dp', 'seq'), may hold values from -6 to 6
Outputs:
- layer_out: bfloat16 [2, 8, 2048, 768], P(None, 'dp', 'seq')
- grad_tokens: float32 [2, 8, 2048, 768], P(None, 'dp', 'seq')
- grad_query_weight: float32 [768, 768], P(('dp', 'seq'))
- grad_query_bias: float32 [768], P(('dp', 'seq'))
- grad_key_weight: float32 [768, 768], P(('dp', 'seq'))
- grad_key_bias: float32 [768], P(('dp', 'seq'))
- grad_value_weight: float32 [768, 768], P(('dp', 'seq'))
- grad_value_bias: float32 [768], P(('dp', 'seq'))
- grad_output_weight: float32 [768, 768], P(('dp', 'seq'))
- grad_output_bias: float32 [768], P(('dp', 'seq'))
- grad_gain_first: float32 [768], P(('dp', 'seq'))
- grad_shift_first: float32 [768], P(('dp', 'seq'))
- grad_inner_weight: float32 [768, 3072], P(('dp', 'seq'))
- grad_inner_bias: float32 [3072], P(('dp', 'seq'))
- grad_outer_weight: float32 [3072, 768], P(('dp', 'seq'))
- grad_outer_bias: float32 [768], P(('dp', 'seq'))
- grad_gain_second: float32 [768], P(('dp', 'seq'))
- grad_shift_second: float32 [768], P(('dp', 'seq'))
Inputs may be any that keep to these rules, and one draw needn't show every extreme that they name: `seq_lengths`: in every micro-batch some sequence has exactly 2048 valid positions; positions at or past a sequence's length are padding.
All inputs are finite; a program needn't handle non-finite values.
Results may differ from a plain program's by a relative error of at most 0.014.
Values may be sent and summed in bfloat16 or wider, within the bound.
No kernel may reach another device: no remote copies, remote signals or barrier semaphores. Data moves between devices by JAX's collectives and lax.ppermute only.
A program may use at most 192 MiB of HBM per device.

v0:
```python
import math
import jax
import jax.numpy as jnp
from jax import lax
from jax.sharding import PartitionSpec as P

H = 12
HD = 64
BLOCK = 512
NORM_EPS = 1e-05
HALF_TURN = math.pi / 2


def layer_norm(values, norm_gain, norm_shift):
    center = values - jnp.mean(values, axis=-1, keepdims=True)
    spread = jnp.mean(center * center, axis=-1, keepdims=True)
    return center * lax.rsqrt(spread + NORM_EPS) * norm_gain + norm_shift


def reweight(places, limit):
    angle = HALF_TURN * places[:, None] / limit[None, :]
    live = (places[:, None] < limit[None, :]).astype(jnp.float32)
    return (jnp.cos(angle) * live, jnp.sin(angle) * live)


def attention(queries, key_rows, values, lengths, offset, initial):
    total_rows, head_count, head_size = queries.shape
    block_rows = min(BLOCK, total_rows)
    block_count = total_rows // block_rows
    limit = lengths.astype(jnp.float32)
    causal = jnp.tril(jnp.ones((block_rows, block_rows), jnp.float32))
    highest = lax.Precision.HIGHEST

    def attend(state_now, inputs):
        sum_cos, sum_sin, norm_cos, norm_sin = state_now
        query_blk, key_blk, value_blk, block_index = inputs
        places = (offset + block_index * block_rows + jnp.arange(block_rows)).astype(jnp.float32)
        weight_cos, weight_sin = reweight(places, limit)
        query_relu = jax.nn.relu(query_blk)
        key_relu = jax.nn.relu(key_blk)
        query_cos = query_relu * weight_cos[:, :, None]
        query_sin = query_relu * weight_sin[:, :, None]
        key_cos = key_relu * weight_cos[:, :, None]
        key_sin = key_relu * weight_sin[:, :, None]
        scores = jnp.einsum("igd,jgd->gij", query_cos, key_cos, precision=highest)
        scores = scores + jnp.einsum("igd,jgd->gij", query_sin, key_sin, precision=highest)
        scores = scores * causal[None, :, :]
        numer = jnp.einsum("gij,jge->ige", scores, value_blk, precision=highest)
        numer = numer + jnp.einsum("igd,gde->ige", query_cos, sum_cos, precision=highest)
        numer = numer + jnp.einsum("igd,gde->ige", query_sin, sum_sin, precision=highest)
        denom = jnp.sum(scores, axis=2).T
        denom = denom + jnp.einsum("igd,gd->ig", query_cos, norm_cos, precision=highest)
        denom = denom + jnp.einsum("igd,gd->ig", query_sin, norm_sin, precision=highest)
        output = numer / jnp.maximum(denom, 1.0)[:, :, None]
        sum_cos = sum_cos + jnp.einsum("jgd,jge->gde", key_cos, value_blk, precision=highest)
        sum_sin = sum_sin + jnp.einsum("jgd,jge->gde", key_sin, value_blk, precision=highest)
        norm_cos = norm_cos + jnp.sum(key_cos, axis=0)
        norm_sin = norm_sin + jnp.sum(key_sin, axis=0)
        return ((sum_cos, sum_sin, norm_cos, norm_sin), output)

    stacked = (
        queries.reshape(block_count, block_rows, head_count, head_size),
        key_rows.reshape(block_count, block_rows, head_count, head_size),
        values.reshape(block_count, block_rows, head_count, head_size),
        jnp.arange(block_count),
    )
    final_state, outputs = lax.scan(jax.checkpoint(attend), initial, stacked)
    return outputs.reshape(total_rows, head_count, head_size)


def make_state(head_count):
    return (
        jnp.zeros((head_count, HD, HD), jnp.float32),
        jnp.zeros((head_count, HD, HD), jnp.float32),
        jnp.zeros((head_count, HD), jnp.float32),
        jnp.zeros((head_count, HD), jnp.float32),
    )


def head_view(packed):
    return packed.astype(jnp.float32)


def per_device(
    tokens,
    seq_lengths,
    query_weight,
    query_bias,
    key_weight,
    key_bias,
    value_weight,
    value_bias,
    output_weight,
    output_bias,
    gain_first,
    shift_first,
    inner_weight,
    inner_bias,
    outer_weight,
    outer_bias,
    gain_second,
    shift_second,
    cotangent,
):
    seq_count = lax.axis_size("seq")
    micro_count, seqs_here, shard_rows, width = tokens.shape
    item_count = seqs_here * H
    item_share = item_count // seq_count
    seq_place = lax.axis_index("seq")
    token_count = seqs_here * shard_rows
    item_index = seq_place * item_share + jnp.arange(item_share)
    head_owner = item_index // H
    owner_match = head_owner[:, None] == jnp.arange(seqs_here)[None, :]
    totals = None
    layer_rows = []
    input_grads = []
    for batch_index in range(micro_count):
        weights_now = (
            lax.all_gather(query_weight, ("dp", "seq"), axis=0, tiled=True),
            lax.all_gather(query_bias, ("dp", "seq"), axis=0, tiled=True),
            lax.all_gather(key_weight, ("dp", "seq"), axis=0, tiled=True),
            lax.all_gather(key_bias, ("dp", "seq"), axis=0, tiled=True),
            lax.all_gather(value_weight, ("dp", "seq"), axis=0, tiled=True),
            lax.all_gather(value_bias, ("dp", "seq"), axis=0, tiled=True),
            lax.all_gather(output_weight, ("dp", "seq"), axis=0, tiled=True),
            lax.all_gather(output_bias, ("dp", "seq"), axis=0, tiled=True),
            lax.all_gather(gain_first, ("dp", "seq"), axis=0, tiled=True),
            lax.all_gather(shift_first, ("dp", "seq"), axis=0, tiled=True),
            lax.all_gather(inner_weight, ("dp", "seq"), axis=0, tiled=True),
            lax.all_gather(inner_bias, ("dp", "seq"), axis=0, tiled=True),
            lax.all_gather(outer_weight, ("dp", "seq"), axis=0, tiled=True),
            lax.all_gather(outer_bias, ("dp", "seq"), axis=0, tiled=True),
            lax.all_gather(gain_second, ("dp", "seq"), axis=0, tiled=True),
            lax.all_gather(shift_second, ("dp", "seq"), axis=0, tiled=True),
        )
        (
            w_query,
            b_query,
            w_key,
            b_key,
            w_value,
            b_value,
            w_output,
            b_output,
            gain_one,
            shift_one,
            w_inner,
            b_inner,
            w_outer,
            b_outer,
            gain_two,
            shift_two,
        ) = weights_now
        lengths_now = seq_lengths[batch_index]
        head_lengths = jnp.sum(jnp.where(owner_match, lengths_now[None, :], 0), axis=1)
        token_now = tokens[batch_index]

        def project(weight_full, bias_full):
            product = jnp.einsum(
                "srd,de->rse", token_now, weight_full, preferred_element_type=jnp.float32
            )
            return (product + bias_full.astype(jnp.float32)).astype(jnp.bfloat16)

        query_low = project(w_query, b_query)
        key_low = project(w_key, b_key)
        value_low = project(w_value, b_value)
        moved = (
            lax.all_to_all(
                query_low.reshape(shard_rows, item_count, HD),
                "seq",
                split_axis=1,
                concat_axis=0,
                tiled=True,
            ),
            lax.all_to_all(
                key_low.reshape(shard_rows, item_count, HD),
                "seq",
                split_axis=1,
                concat_axis=0,
                tiled=True,
            ),
            lax.all_to_all(
                value_low.reshape(shard_rows, item_count, HD),
                "seq",
                split_axis=1,
                concat_axis=0,
                tiled=True,
            ),
        )
        zero_state = make_state(item_share)

        def core_heads(query_in, key_in, value_in):
            return attention(query_in, key_in, value_in, head_lengths, 0, zero_state)

        mixed_heads, attention_pull = jax.vjp(
            core_heads, head_view(moved[0]), head_view(moved[1]), head_view(moved[2])
        )
        mixed_send = mixed_heads.astype(jnp.bfloat16)
        mixed_low = lax.all_to_all(
            mixed_send, "seq", split_axis=0, concat_axis=1, tiled=True
        ).reshape(shard_rows, seqs_here, width)
        attended = jnp.einsum(
            "rse,ef->srf", mixed_low, w_output, preferred_element_type=jnp.float32
        )
        attended = attended + b_output.astype(jnp.float32)
        resid_one = token_now.astype(jnp.float32) + attended
        first, norm_one_pull = jax.vjp(
            layer_norm, resid_one, gain_one.astype(jnp.float32), shift_one.astype(jnp.float32)
        )
        first_flat = first.reshape(token_count, width)
        first_low = first_flat.astype(jnp.bfloat16)
        inner = jnp.dot(first_low, w_inner, preferred_element_type=jnp.float32) + b_inner.astype(
            jnp.float32
        )
        hidden_full, gelu_pull = jax.vjp(jax.nn.gelu, inner)
        hidden = hidden_full.astype(jnp.bfloat16)
        outer = jnp.dot(hidden, w_outer, preferred_element_type=jnp.float32) + b_outer.astype(
            jnp.float32
        )
        final, norm_two_pull = jax.vjp(
            layer_norm,
            first_flat + outer,
            gain_two.astype(jnp.float32),
            shift_two.astype(jnp.float32),
        )
        layer_rows.append(final.astype(jnp.bfloat16).reshape(seqs_here, shard_rows, width))
        grad_final = cotangent[batch_index].astype(jnp.float32).reshape(token_count, width)
        d_second, grad_gain_two, grad_shift_two = norm_two_pull(grad_final)
        d_outer = d_second.astype(jnp.bfloat16)
        grad_w_outer = jnp.einsum("nf,nd->fd", hidden, d_outer, preferred_element_type=jnp.float32)
        grad_b_outer = jnp.sum(d_outer, axis=0, dtype=jnp.float32)
        d_hidden = jnp.einsum("nd,fd->nf", d_outer, w_outer, preferred_element_type=jnp.float32)
        (d_inner_full,) = gelu_pull(d_hidden)
        d_inner = d_inner_full.astype(jnp.bfloat16)
        grad_w_inner = jnp.einsum(
            "nd,nf->df", first_low, d_inner, preferred_element_type=jnp.float32
        )
        grad_b_inner = jnp.sum(d_inner, axis=0, dtype=jnp.float32)
        d_first = d_second + jnp.einsum(
            "nf,df->nd", d_inner, w_inner, preferred_element_type=jnp.float32
        )
        d_resid, grad_gain_one, grad_shift_one = norm_one_pull(
            d_first.reshape(seqs_here, shard_rows, width)
        )
        d_attended = d_resid.astype(jnp.bfloat16)
        grad_w_output = jnp.einsum(
            "rse,srf->ef", mixed_low, d_attended, preferred_element_type=jnp.float32
        )
        grad_b_output = jnp.sum(d_attended, axis=(0, 1), dtype=jnp.float32)
        d_mixed = jnp.einsum(
            "srf,ef->rse", d_attended, w_output, preferred_element_type=jnp.float32
        ).astype(jnp.bfloat16)
        d_heads = lax.all_to_all(
            d_mixed.reshape(shard_rows, item_count, HD),
            "seq",
            split_axis=1,
            concat_axis=0,
            tiled=True,
        )
        d_query_heads, d_key_heads, d_value_heads = attention_pull(head_view(d_heads))
        returned = (
            lax.all_to_all(
                d_query_heads.astype(jnp.bfloat16), "seq", split_axis=0, concat_axis=1, tiled=True
            ),
            lax.all_to_all(
                d_key_heads.astype(jnp.bfloat16), "seq", split_axis=0, concat_axis=1, tiled=True
            ),
            lax.all_to_all(
                d_value_heads.astype(jnp.bfloat16), "seq", split_axis=0, concat_axis=1, tiled=True
            ),
        )
        d_query = returned[0].reshape(shard_rows, seqs_here, width)
        d_key = returned[1].reshape(shard_rows, seqs_here, width)
        d_value = returned[2].reshape(shard_rows, seqs_here, width)
        grad_w_query = jnp.einsum(
            "srd,rse->de", token_now, d_query, preferred_element_type=jnp.float32
        )
        grad_w_key = jnp.einsum("srd,rse->de", token_now, d_key, preferred_element_type=jnp.float32)
        grad_w_value = jnp.einsum(
            "srd,rse->de", token_now, d_value, preferred_element_type=jnp.float32
        )
        grad_b_query = jnp.sum(d_query, axis=(0, 1), dtype=jnp.float32)
        grad_b_key = jnp.sum(d_key, axis=(0, 1), dtype=jnp.float32)
        grad_b_value = jnp.sum(d_value, axis=(0, 1), dtype=jnp.float32)
        d_tokens = d_resid + jnp.einsum(
            "rse,de->srd", d_query, w_query, preferred_element_type=jnp.float32
        )
        d_tokens = d_tokens + jnp.einsum(
            "rse,de->srd", d_key, w_key, preferred_element_type=jnp.float32
        )
        d_tokens = d_tokens + jnp.einsum(
            "rse,de->srd", d_value, w_value, preferred_element_type=jnp.float32
        )
        input_grads.append(d_tokens)
        batch_grads = (
            grad_w_query,
            grad_b_query,
            grad_w_key,
            grad_b_key,
            grad_w_value,
            grad_b_value,
            grad_w_output,
            grad_b_output,
            grad_gain_one,
            grad_shift_one,
            grad_w_inner,
            grad_b_inner,
            grad_w_outer,
            grad_b_outer,
            grad_gain_two,
            grad_shift_two,
        )
        if totals is None:
            totals = batch_grads
        else:
            totals = jax.tree.map(jnp.add, totals, batch_grads)
    shards = (
        lax.psum_scatter(totals[0], ("dp", "seq"), scatter_dimension=0, tiled=True),
        lax.psum_scatter(totals[1], ("dp", "seq"), scatter_dimension=0, tiled=True),
        lax.psum_scatter(totals[2], ("dp", "seq"), scatter_dimension=0, tiled=True),
        lax.psum_scatter(totals[3], ("dp", "seq"), scatter_dimension=0, tiled=True),
        lax.psum_scatter(totals[4], ("dp", "seq"), scatter_dimension=0, tiled=True),
        lax.psum_scatter(totals[5], ("dp", "seq"), scatter_dimension=0, tiled=True),
        lax.psum_scatter(totals[6], ("dp", "seq"), scatter_dimension=0, tiled=True),
        lax.psum_scatter(totals[7], ("dp", "seq"), scatter_dimension=0, tiled=True),
        lax.psum_scatter(totals[8], ("dp", "seq"), scatter_dimension=0, tiled=True),
        lax.psum_scatter(totals[9], ("dp", "seq"), scatter_dimension=0, tiled=True),
        lax.psum_scatter(totals[10], ("dp", "seq"), scatter_dimension=0, tiled=True),
        lax.psum_scatter(totals[11], ("dp", "seq"), scatter_dimension=0, tiled=True),
        lax.psum_scatter(totals[12], ("dp", "seq"), scatter_dimension=0, tiled=True),
        lax.psum_scatter(totals[13], ("dp", "seq"), scatter_dimension=0, tiled=True),
        lax.psum_scatter(totals[14], ("dp", "seq"), scatter_dimension=0, tiled=True),
        lax.psum_scatter(totals[15], ("dp", "seq"), scatter_dimension=0, tiled=True),
    )
    return (jnp.stack(layer_rows), jnp.stack(input_grads)) + tuple(shards)


def solution(mesh):
    in_specs = (
        P(None, "dp", "seq", None),
        P(None, "dp"),
        P(("dp", "seq"), None),
        P(("dp", "seq")),
        P(("dp", "seq"), None),
        P(("dp", "seq")),
        P(("dp", "seq"), None),
        P(("dp", "seq")),
        P(("dp", "seq"), None),
        P(("dp", "seq")),
        P(("dp", "seq")),
        P(("dp", "seq")),
        P(("dp", "seq"), None),
        P(("dp", "seq")),
        P(("dp", "seq"), None),
        P(("dp", "seq")),
        P(("dp", "seq")),
        P(("dp", "seq")),
        P(None, "dp", "seq", None),
    )
    out_specs = (
        P(None, "dp", "seq", None),
        P(None, "dp", "seq", None),
        P(("dp", "seq"), None),
        P(("dp", "seq")),
        P(("dp", "seq"), None),
        P(("dp", "seq")),
        P(("dp", "seq"), None),
        P(("dp", "seq")),
        P(("dp", "seq"), None),
        P(("dp", "seq")),
        P(("dp", "seq")),
        P(("dp", "seq")),
        P(("dp", "seq"), None),
        P(("dp", "seq")),
        P(("dp", "seq"), None),
        P(("dp", "seq")),
        P(("dp", "seq")),
        P(("dp", "seq")),
    )
    return jax.shard_map(
        per_device, mesh=mesh, in_specs=in_specs, out_specs=out_specs, check_vma=False
    )
```

profile of v0, /device:TPU:0, one launch (start us, length us, event | category | flops | bytes accessed | tf_op | source)
XLA Modules:
  0.0 1656.1 jit_solution(1364522023092862360)
XLA Ops:
  19.0 42.7 %all-reduce.21 = (bf16[768]{0:T(1024)(128)(2,1)S(1)}, bf16[768]{0:T(1024)(128)(2,1)S(1)}, bf16[768]{0:T(1024)(128)(2,1)S(1)}, bf16[768]{0:T(1024)(128)(2,1)}, bf...) all-reduce(bf16[768]{0:T(1024)(128)(2,1)S(1)} %dynamic-update-slice, ...), channel_id=1, replica_groups=mesh['dp'=8,'seq'=4] {'dp','seq'}, use_global_device_ids=true, to_apply=%add | all-reduce | flops 9984 | bytes 39936
  74.6 53.0 %all-gather.7.cloned.1.call-done = bf16[768,768]{1,0:T(8,128)(2,1)} async-done(((bf16[24,768]{1,0:T(8,128)(2,1)}), bf16[768,768]{1,0:T(8,128)(2,1)}) %all-gather.7.cloned.1.call-update) | async-done | bytes 1179664 | tf_op jit(solution)/shard_map/all_gather | solution.py:121
  134.8 52.8 %all-gather.11.cloned.1.call-done = bf16[768,768]{1,0:T(8,128)(2,1)} async-done(((bf16[24,768]{1,0:T(8,128)(2,1)}), bf16[768,768]{1,0:T(8,128)(2,1)}) %all-gather.11.cloned.1.call-update) | async-done | bytes 1179664 | tf_op jit(solution)/shard_map/all_gather | solution.py:119
  196.6 19.9 %all-to-all-done.6 = bf16[512,12,64]{0,2,1:T(8,128)(2,1)} async-done(((bf16[512,12,64]{0,2,1:T(8,128)(2,1)}), bf16[512,12,64]{0,2,1:T(8,128)(2,1)}, u32[]{:S(2)}, u32[]{:S(2)}) %all-to-all-start.6) | async-done | bytes 786464 | tf_op jit(solution)/shard_map/all_to_all | solution.py:168
  223.6 17.4 %all-to-all-done.1 = bf16[512,12,64]{0,2,1:T(8,128)(2,1)S(1)} async-done(((bf16[512,12,64]{0,2,1:T(8,128)(2,1)}), bf16[512,12,64]{0,2,1:T(8,128)(2,1)S(1)}, u32[]{:S(2)}, u32[]{:S(2)}) %all-to-all-start.1) | async-done | bytes 786464 | tf_op jit(solution)/shard_map/all_to_all | solution.py:182
  254.7 11.4 all-to-all-done
  274.3 109.1 %while.111 = (s32[]{:T(128)}, f32[3,64,64]{2,1,0:T(8,128)S(1)}, f32[3,64,64]{2,1,0:T(8,128)S(1)}, f32[3,64]{1,0:T(4,128)}, f32[3,64]{1,0:T(4,128)}, /*index=5*/b...) while((s32[]{:T(128)}, f32[3,64,64]{2,1,0:T(8,128)S(1)}, ...), condition=%wide.region_13.14_spmd.clone, body=%wide.region_9.13_spmd.clone.sunk | while | flops 2122035456 | bytes 35606024 | solution.py:67
  402.3 92.9 %while.110 = (s32[]{:T(128)}, f32[3,64,64]{2,1,0:T(8,128)S(1)}, f32[3,64,64]{2,1,0:T(8,128)S(1)}, f32[3,64]{1,0:T(4,128)S(1)}, f32[3,64]{1,0:T(4,128)S(1)}, /*in...) while((s32[]{:T(128)}, f32[3,64,64]{2,1,0:T(8,128)S(1)}, ...), condition=%wide.region_4.5_spmd.clone, body=%wide.region_0.0_spmd.clone.sunk | while | flops 2122035456 | bytes 35605332 | solution.py:67
  511.2 13.5 all-to-all-done.3
  544.9 7.9 fusion.404
  573.3 18.0 %convert_reduce_fusion.1 = (f32[3072]{0:T(1024)}, bf16[512,3072]{1,0:T(8,128)(2,1)}, f32[3072]{0:T(1024)}, bf16[512,3072]{1,0:T(8,128)(2,1)S(1)}) fusion(f32[512,3072]{1,0:T(8,128)} %copy-done.110, f32[3072]{0:T(1024)S(1)} %convert_element_type.481, f32[512,3072]{1,0:T(8,128)} %fusion.410, f32[512,3072]{1,0:T(8,128)} %fusion.388, ...), kind=kOutput, calls=%fused_computation.463 | convolution fusion | flops 2488264704 | bytes 30707712 | tf_op jit(solution)/shard_map/nd,fd->nf/dot_general | solution.py:232
  616.4 11.5 all-to-all-done.8
  636.5 173.0 %while.112 = (s32[]{:T(128)}, f32[3,64,64]{2,1,0:T(8,128)S(1)}, f32[3,64,64]{2,1,0:T(8,128)S(1)}, f32[3,64]{1,0:T(4,128)S(1)}, f32[3,64]{1,0:T(4,128)S(1)}, /*in...) while((s32[]{:T(128)}, f32[3,64,64]{2,1,0:T(8,128)S(1)}, ...), condition=%wide.region_25.26_spmd.clone, body=%wide.region_22.25_spmd.clone.sunk | while | flops 6211543040 | bytes 82320360 | solution.py:67
  825.4 183.5 %while.113 = (s32[]{:T(128)}, f32[3,64,64]{2,1,0:T(8,128)S(1)}, f32[3,64,64]{2,1,0:T(8,128)S(1)}, f32[3,64]{1,0:T(4,128)S(1)}, f32[3,64]{1,0:T(4,128)S(1)}, /*in...) while((s32[]{:T(128)}, f32[3,64,64]{2,1,0:T(8,128)S(1)}, ...), condition=%wide.region_33.34_spmd.clone, body=%wide.region_30.33_spmd.clone.sunk | while | flops 6211543040 | bytes 82320360 | solution.py:67
  1024.5 13.5 all-to-all-done.15
  1071.6 11.5 all-to-all-done.10
  1095.4 17.3 %all-to-all-done.14 = bf16[4,2,49152]{2,1,0:T(2,128)(2,1)} async-done(((bf16[4,2,49152]{2,1,0:T(2,128)(2,1)}), bf16[4,2,49152]{2,1,0:T(2,128)(2,1)}, u32[]{:S(2)}, u32[]{:S(2)}) %all-to-all-start.14) | async-done | bytes 786464 | tf_op jit(solution)/shard_map/all_to_all | solution.py:265
  1149.2 11.8 all-to-all-done.9
  1173.3 11.6 all-to-all-done.13
  1207.8 10.5 convolution_add_fusion.24
  1262.7 38.7 %all-reduce.20 = (f32[768]{0:T(1024)S(1)}, f32[768]{0:T(1024)S(1)}, f32[768]{0:T(1024)S(1)}, f32[768]{0:T(1024)S(1)}, f32[768]{0:T(1024)S(1)}, /*index=5*/f32[76...) all-reduce(f32[768]{0:T(1024)S(1)} %add.724, ...), channel_id=3, replica_groups=mesh['dp'=8,'seq'=4] {'dp','seq'}, use_global_device_ids=true, to_apply=%region_37.38.clone | all-reduce | flops 9984 | bytes 79872
  1319.1 46.5 %reduce-scatter.19.cloned.1.call-done = f32[24,768]{1,0:T(8,128)} async-done(((f32[768,768]{1,0:T(8,128)}), f32[24,768]{1,0:T(8,128)}) %reduce-scatter.19.cloned.1.call-update) | async-done | bytes 73744
  1365.5 141.8 %reduce-scatter.17.cloned.1.call-done = f32[96,768]{1,0:T(8,128)} async-done(((f32[3072,768]{1,0:T(8,128)}), f32[96,768]{1,0:T(8,128)}) %reduce-scatter.17.cloned.1.call-update) | async-done | bytes 294928 | tf_op jit(solution)/shard_map/reduce_scatter | solution.py:330
  1507.3 141.4 %reduce-scatter.15.cloned.1.call-done = f32[24,3072]{1,0:T(8,128)} async-done(((f32[768,3072]{1,0:T(8,128)}), f32[24,3072]{1,0:T(8,128)}) %reduce-scatter.15.cloned.1.call-update) | async-done | bytes 294928 | tf_op jit(solution)/shard_map/reduce_scatter | solution.py:328
  (1087 shorter events, 887.0 us)
Async XLA Ops:
  7.2 60.5 %all-gather.9.cloned.1.call-start = ((), (), s32[]{:S(2)}) async-start(), calls=%async_computation.23 | async-start | bytes 1216512 | tf_op jit(solution)/shard_map/all_gather | solution.py:123
  7.9 119.6 %all-gather.7.cloned.1.call-start = ((), (), s32[]{:S(2)}) async-start(), calls=%async_computation.22 | async-start | bytes 1216512 | tf_op jit(solution)/shard_map/all_gather | solution.py:121
  8.7 178.9 %all-gather.11.cloned.1.call-start = ((), (), s32[]{:S(2)}) async-start(), calls=%async_computation.24 | async-start | bytes 1216512 | tf_op jit(solution)/shard_map/all_gather | solution.py:119
  9.4 521.8 %all-gather.13.cloned.1.call-start = ((), (), s32[]{:S(2)}) async-start(), calls=%async_computation.25 | async-start | bytes 1216512 | tf_op jit(solution)/shard_map/all_gather | solution.py:125
  10.0 528.0 %all-gather.15.cloned.1.call-start = ((), (), s32[]{:S(2)}) async-start(), calls=%async_computation.26 | async-start | bytes 4866048 | tf_op jit(solution)/shard_map/all_gather | solution.py:129
  70.9 59.6 %all-to-all-start.5 = ((bf16[512,12,64]{0,2,1:T(8,128)(2,1)}), bf16[512,12,64]{0,2,1:T(8,128)(2,1)S(1)}, u32[]{:S(2)}, u32[]{:S(2)}) async-start(bf16[512,12,64]{0,2,1:T(8,128)(2,1)} %bitcast.37), calls=%async_computation.5 | async-start | bytes 1572864 | tf_op jit(solution)/shard_map/all_to_all | solution.py:182
  130.6 60.0 %all-to-all-start.4 = ((bf16[512,12,64]{0,2,1:T(8,128)(2,1)}), bf16[512,12,64]{0,2,1:T(8,128)(2,1)}, u32[]{:S(2)}, u32[]{:S(2)}) async-start(bf16[512,12,64]{0,2,1:T(8,128)(2,1)} %bitcast.32), calls=%async_computation.4 | async-start | bytes 1572864 | tf_op jit(solution)/shard_map/all_to_all | solution.py:175
  190.6 26.0 %all-to-all-start.6 = ((bf16[512,12,64]{0,2,1:T(8,128)(2,1)}), bf16[512,12,64]{0,2,1:T(8,128)(2,1)}, u32[]{:S(2)}, u32[]{:S(2)}) async-start(bf16[512,12,64]{0,2,1:T(8,128)(2,1)} %bitcast.1129), calls=%async_computation.6 | async-start | bytes 1572864 | tf_op jit(solution)/shard_map/all_to_all | solution.py:168
  216.5 24.5 %all-to-all-start.1 = ((bf16[512,12,64]{0,2,1:T(8,128)(2,1)}), bf16[512,12,64]{0,2,1:T(8,128)(2,1)S(1)}, u32[]{:S(2)}, u32[]{:S(2)}) async-start(bf16[512,12,64]{0,2,1:T(8,128)(2,1)} %bitcast.1128), calls=%async_computation.1 | async-start | bytes 1572864 | tf_op jit(solution)/shard_map/all_to_all | solution.py:182
  220.0 324.9 %all-gather.17.cloned.1.call-start = ((), (), s32[]{:S(2)}) async-start(), calls=%async_computation.27 | async-start | bytes 4866048 | tf_op jit(solution)/shard_map/all_gather | solution.py:131
  241.0 25.1 %all-to-all-start = ((bf16[512,12,64]{0,2,1:T(8,128)(2,1)}), bf16[512,12,64]{0,2,1:T(8,128)(2,1)S(1)}, u32[]{:S(2)}, u32[]{:S(2)}) async-start(bf16[512,12,64]{0,2,1:T(8,128)(2,1)} %bitcast.1127), calls=%async_computation | async-start | bytes 1572864 | tf_op jit(solution)/shard_map/all_to_all | solution.py:175
  266.1 125.5 %all-to-all-start.2 = ((bf16[512,12,64]{0,2,1:T(8,128)(2,1)}), bf16[512,12,64]{0,2,1:T(8,128)(2,1)}, u32[]{:S(2)}, u32[]{:S(2)}) async-start(bf16[512,12,64]{0,2,1:T(8,128)(2,1)} %bitcast.14), calls=%async_computation.2 | async-start | bytes 1572864 | tf_op jit(solution)/shard_map/all_to_all | solution.py:168
  391.5 109.1 %all-to-all-start.7 = ((bf16[4,2,49152]{2,1,0:T(2,128)(2,1)}), bf16[4,2,49152]{2,1,0:T(2,128)(2,1)}, u32[]{:S(2)}, u32[]{:S(2)}) async-start(bf16[4,2,49152]{2,1,0:T(2,128)(2,1)} %reshape.1161), calls=%async_computation.7 | async-start | bytes 1572864 | tf_op jit(solution)/shard_map/all_to_all | solution.py:199
  500.6 24.1 %all-to-all-start.3 = ((bf16[4,2,49152]{2,1,0:T(2,128)(2,1)}), bf16[4,2,49152]{2,1,0:T(2,128)(2,1)S(1)}, u32[]{:S(2)}, u32[]{:S(2)}) async-start(bf16[4,2,49152]{2,1,0:T(2,128)(2,1)} %reshape.1163), calls=%async_computation.3 | async-start | bytes 1572864 | tf_op jit(solution)/shard_map/all_to_all | solution.py:199
  608.3 710.8 %reduce-scatter.13.cloned.1.call-start = ((), (), s32[]{:S(2)}) async-start(), calls=%async_computation.28 | async-start | bytes 2433024 | tf_op jit(solution)/shard_map/reduce_scatter | solution.py:324
  627.9 187.0 %all-to-all-start.12 = ((bf16[512,12,64]{0,2,1:T(8,128)(2,1)}), bf16[512,12,64]{0,2,1:T(8,128)(2,1)}, u32[]{:S(2)}, u32[]{:S(2)}) async-start(bf16[512,12,64]{0,2,1:T(8,128)(2,1)} %bitcast.104), calls=%async_computation.12 | async-start | bytes 1572864 | tf_op jit(solution)/shard_map/all_to_all | solution.py:253
  814.9 199.4 %all-to-all-start.11 = ((bf16[4,2,49152]{2,1,0:T(2,128)(2,1)}), bf16[4,2,49152]{2,1,0:T(2,128)(2,1)}, u32[]{:S(2)}, u32[]{:S(2)}) async-start(bf16[4,2,49152]{2,1,0:T(2,128)(2,1)} %reshape.1175), calls=%async_computation.11 | async-start | bytes 1572864 | tf_op jit(solution)/shard_map/all_to_all | solution.py:268
  1019.4 299.7 %reduce-scatter.23.cloned.1.call-start = ((), (), s32[]{:S(2)}) async-start(), calls=%async_computation.33 | async-start | bytes 2433024
  1083.1 29.6 %all-to-all-start.14 = ((bf16[4,2,49152]{2,1,0:T(2,128)(2,1)}), bf16[4,2,49152]{2,1,0:T(2,128)(2,1)}, u32[]{:S(2)}, u32[]{:S(2)}) async-start(bf16[4,2,49152]{2,1,0:T(2,128)(2,1)} %reshape.1165), calls=%async_computation.14 | async-start | bytes 1572864 | tf_op jit(solution)/shard_map/all_to_all | solution.py:265
  1087.3 231.7 %reduce-scatter.21.cloned.1.call-start = ((), (), s32[]{:S(2)}) async-start(), calls=%async_computation.32 | async-start | bytes 2433024
  1136.8 24.2 %all-to-all-start.9 = ((bf16[4,2,49152]{2,1,0:T(2,128)(2,1)}), bf16[4,2,49152]{2,1,0:T(2,128)(2,1)}, u32[]{:S(2)}, u32[]{:S(2)}) async-start(bf16[4,2,49152]{2,1,0:T(2,128)(2,1)} %reshape.1173), calls=%async_computation.9 | async-start | bytes 1572864 | tf_op jit(solution)/shard_map/all_to_all | solution.py:262
  1165.2 200.3 %reduce-scatter.19.cloned.1.call-start = ((), (), s32[]{:S(2)}) async-start(), calls=%async_computation.31 | async-start | bytes 2433024
  1200.7 306.5 %reduce-scatter.17.cloned.1.call-start = ((), (), s32[]{:S(2)}) async-start(), calls=%async_computation.30 | async-start | bytes 9732096 | tf_op jit(solution)/shard_map/reduce_scatter | solution.py:330
  1218.3 430.4 %reduce-scatter.15.cloned.1.call-start = ((), (), s32[]{:S(2)}) async-start(), calls=%async_computation.29 | async-start | bytes 9732096 | tf_op jit(solution)/shard_map/reduce_scatter | solution.py:328
  (178 other events, 1316.8 us)
Sparse Core Ops, SparseCore 0:
  10.8 56.8 all-gather.8
  70.5 57.0 all-gather.6
  130.4 57.1 all-gather.10
  190.2 65.9 all-gather.12
  258.8 71.8 all-gather.14
  333.3 61.7 all-gather.16
  615.0 100.7 reduce-scatter.12
  1051.0 100.6 reduce-scatter.22
  1157.6 103.5 reduce-scatter.20
  1266.9 98.6 reduce-scatter.18
  1372.0 135.2 reduce-scatter.16
  1513.6 135.0 reduce-scatter.14
where the time goes:
time: 1670 us; the launch traced here: 1660 us
  waiting for transfers between devices  585 us (35%)
  matrix products  537 us (32%)
  local copies, waits for them, and re-layouts  221 us (13%)
  other arithmetic  86.3 us (5%)
  blocking collectives  81.3 us (5%)
  starting transfers between devices  69.6 us (4%)
  loops' own time  60.4 us (4%)
    reduce_scatter x1, waiting for transfers between devices, per_device(): lax.psum_scatter(totals[12], ('dp', 'seq'), scatter_dimension=0, tiled=True)  142 us
    reduce_scatter x1, waiting for transfers between devices, per_device(): lax.psum_scatter(totals[10], ('dp', 'seq'), scatter_dimension=0, tiled=True)  141 us
    dot_general x32, matrix products, attend(): jnp.einsum('igd,jgd->gij', query_sin, key_sin, precision=highest)  107 us
    dot_general x32, matrix products, attend(): scores = jnp.einsum('igd,jgd->gij', query_cos, key_cos, precision=highest)  99.1 us
    unnamed x237, local copies, waits for them, and re-layouts  89.4 us
    unnamed x2, blocking collectives  81.3 us
    dot_general x32, matrix products, attend(): numer = jnp.einsum('gij,jge->ige', scores, value_blk, precision=highest)  79.1 us
    another operation x4, loops' own time, attention(): final_state, outputs = lax.scan(jax.checkpoint(attend), initial, stacked)  60.4 us
  transfers between devices with their start and end apart: 28, of which 16 were waited for; matrix products, arithmetic and copies ran while one was open for 47% of the time, Pallas kernels for 0%

commit v1 on v0

--- a/solution.py
+++ b/solution.py
@@ -259,8 +259,16 @@
         )
         d_query_heads, d_key_heads, d_value_heads = attention_pull(head_view(d_heads))
         returned = (
-            lax.all_to_all(
-                d_query_heads.astype(jnp.bfloat16), "seq", split_axis=0, concat_axis=1, tiled=True
+            jnp.concatenate(
+                lax.all_to_all(
+                    jnp.stack(
+                        jnp.split(d_query_heads.astype(jnp.bfloat16), lax.axis_size("seq"), axis=0)
+                    ),
+                    "seq",
+                    0,
+                    0,
+                ),
+                axis=1,
             ),
             lax.all_to_all(
                 d_key_heads.astype(jnp.bfloat16), "seq", split_axis=0, concat_axis=1, tiled=True

time: 1670 us -> 1660 us (level)
  local copies, waits for them, and re-layouts: 221 us -> 181 us
  blocking collectives: 81.3 us -> 105 us
    all_to_all x0 -> x1, blocking collectives: none -> 24.6 us  [per_device(): lax.all_to_all(jnp.stack(jnp.split(d_query_heads.astype(jnp.bfloat16), la...]
    unnamed x237 -> x227, local copies, waits for them, and re-layouts: 89.4 us -> 71.2 us
    unnamed x15, waiting for transfers between devices: 50.2 us -> 68.4 us
  transfers between devices with their start and end apart: 28 -> 27, of which waited for: 16 -> 15; matrix products, arithmetic and copies ran while one was open for 47% -> 45% of each run, Pallas kernels for 0% -> 0%
where the time goes in v1:
time: 1660 us; the launch traced here: 1650 us
  waiting for transfers between devices  595 us (36%)
  matrix products  542 us (33%)
  local copies, waits for them, and re-layouts  181 us (11%)
  blocking collectives  105 us (6%)
  other arithmetic  86.3 us (5%)
  starting transfers between devices  65.3 us (4%)
  loops' own time  59 us (4%)
    reduce_scatter x1, waiting for transfers between devices, per_device(): lax.psum_scatter(totals[12], ('dp', 'seq'), scatter_dimension=0, tiled=True)  142 us
    reduce_scatter x1, waiting for transfers between devices, per_device(): lax.psum_scatter(totals[10], ('dp', 'seq'), scatter_dimension=0, tiled=True)  141 us
    dot_general x32, matrix products, attend(): jnp.einsum('igd,jgd->gij', query_sin, key_sin, precision=highest)  107 us
    dot_general x32, matrix products, attend(): scores = jnp.einsum('igd,jgd->gij', query_cos, key_cos, precision=highest)  99.1 us
    unnamed x2, blocking collectives  80.8 us
    dot_general x32, matrix products, attend(): numer = jnp.einsum('gij,jge->ige', scores, value_blk, precision=highest)  79.1 us
    unnamed x227, local copies, waits for them, and re-layouts  71.2 us
    unnamed x15, waiting for transfers between devices  68.4 us
  transfers between devices with their start and end apart: 27, of which 15 were waited for; matrix products, arithmetic and copies ran while one was open for 45% of the time, Pallas kernels for 0%

profile of v1, /device:TPU:0, one launch (start us, length us, event | category | flops | bytes accessed | tf_op | source)
XLA Modules:
  0.0 1650.3 jit_solution(3359227789678907376)
XLA Ops:
  19.0 42.7 %all-reduce.21 = (bf16[768]{0:T(1024)(128)(2,1)S(1)}, bf16[768]{0:T(1024)(128)(2,1)S(1)}, bf16[768]{0:T(1024)(128)(2,1)S(1)}, bf16[768]{0:T(1024)(128)(2,1)}, bf...) all-reduce(bf16[768]{0:T(1024)(128)(2,1)S(1)} %dynamic-update-slice, ...), channel_id=1, replica_groups=mesh['dp'=8,'seq'=4] {'dp','seq'}, use_global_device_ids=true, to_apply=%add | all-reduce | flops 9984 | bytes 39936
  74.6 52.9 %all-gather.7.cloned.1.call-done = bf16[768,768]{1,0:T(8,128)(2,1)} async-done(((bf16[24,768]{1,0:T(8,128)(2,1)}), bf16[768,768]{1,0:T(8,128)(2,1)}) %all-gather.7.cloned.1.call-update) | async-done | bytes 1179664 | tf_op jit(solution)/shard_map/all_gather | solution.py:121
  134.7 52.8 %all-gather.11.cloned.1.call-done = bf16[768,768]{1,0:T(8,128)(2,1)} async-done(((bf16[24,768]{1,0:T(8,128)(2,1)}), bf16[768,768]{1,0:T(8,128)(2,1)}) %all-gather.11.cloned.1.call-update) | async-done | bytes 1179664 | tf_op jit(solution)/shard_map/all_gather | solution.py:119
  196.6 19.9 %all-to-all-done.6 = bf16[512,12,64]{0,2,1:T(8,128)(2,1)} async-done(((bf16[512,12,64]{0,2,1:T(8,128)(2,1)}), bf16[512,12,64]{0,2,1:T(8,128)(2,1)}, u32[]{:S(2)}, u32[]{:S(2)}) %all-to-all-start.6) | async-done | bytes 786464 | tf_op jit(solution)/shard_map/all_to_all | solution.py:168
  223.6 17.3 %all-to-all-done.1 = bf16[512,12,64]{0,2,1:T(8,128)(2,1)S(1)} async-done(((bf16[512,12,64]{0,2,1:T(8,128)(2,1)}), bf16[512,12,64]{0,2,1:T(8,128)(2,1)S(1)}, u32[]{:S(2)}, u32[]{:S(2)}) %all-to-all-start.1) | async-done | bytes 786464 | tf_op jit(solution)/shard_map/all_to_all | solution.py:182
  254.6 11.3 all-to-all-done
  274.2 109.7 %while.111 = (s32[]{:T(128)}, f32[3,64,64]{2,1,0:T(8,128)S(1)}, f32[3,64,64]{2,1,0:T(8,128)S(1)}, f32[3,64]{1,0:T(4,128)}, f32[3,64]{1,0:T(4,128)}, /*index=5*/b...) while((s32[]{:T(128)}, f32[3,64,64]{2,1,0:T(8,128)S(1)}, ...), condition=%wide.region_13.14_spmd.clone, body=%wide.region_9.13_spmd.clone.sunk | while | flops 2122035456 | bytes 35606024 | solution.py:67
  402.7 92.9 %while.110 = (s32[]{:T(128)}, f32[3,64,64]{2,1,0:T(8,128)S(1)}, f32[3,64,64]{2,1,0:T(8,128)S(1)}, f32[3,64]{1,0:T(4,128)S(1)}, f32[3,64]{1,0:T(4,128)S(1)}, /*in...) while((s32[]{:T(128)}, f32[3,64,64]{2,1,0:T(8,128)S(1)}, ...), condition=%wide.region_4.5_spmd.clone, body=%wide.region_0.0_spmd.clone.sunk | while | flops 2122035456 | bytes 35605332 | solution.py:67
  511.6 13.5 all-to-all-done.3
  545.4 7.9 fusion.404
  573.7 18.0 %convert_reduce_fusion.1 = (f32[3072]{0:T(1024)}, bf16[512,3072]{1,0:T(8,128)(2,1)}, f32[3072]{0:T(1024)}, bf16[512,3072]{1,0:T(8,128)(2,1)S(1)}) fusion(f32[512,3072]{1,0:T(8,128)} %copy-done.107, f32[3072]{0:T(1024)S(1)} %convert_element_type.477, f32[512,3072]{1,0:T(8,128)} %fusion.410, f32[512,3072]{1,0:T(8,128)} %fusion.388, ...), kind=kOutput, calls=%fused_computation.463 | convolution fusion | flops 2488264704 | bytes 30707712 | tf_op jit(solution)/shard_map/nd,fd->nf/dot_general | solution.py:232
  616.8 11.5 all-to-all-done.8
  636.9 173.0 %while.112 = (s32[]{:T(128)}, f32[3,64,64]{2,1,0:T(8,128)S(1)}, f32[3,64,64]{2,1,0:T(8,128)S(1)}, f32[3,64]{1,0:T(4,128)S(1)}, f32[3,64]{1,0:T(4,128)S(1)}, /*in...) while((s32[]{:T(128)}, f32[3,64,64]{2,1,0:T(8,128)S(1)}, ...), condition=%wide.region_25.26_spmd.clone, body=%wide.region_22.25_spmd.clone.sunk | while | flops 6211543040 | bytes 82320360 | solution.py:67
  825.8 182.2 %while.113 = (s32[]{:T(128)}, f32[3,64,64]{2,1,0:T(8,128)S(1)}, f32[3,64,64]{2,1,0:T(8,128)S(1)}, f32[3,64]{1,0:T(4,128)S(1)}, f32[3,64]{1,0:T(4,128)S(1)}, /*in...) while((s32[]{:T(128)}, f32[3,64,64]{2,1,0:T(8,128)S(1)}, ...), condition=%wide.region_33.34_spmd.clone, body=%wide.region_30.33_spmd.clone.sunk | while | flops 6211543040 | bytes 82320360 | solution.py:67
  1023.5 13.5 all-to-all-done.15
  1070.7 11.5 all-to-all-done.10
  1094.5 17.4 %all-to-all-done.14 = bf16[4,2,49152]{2,1,0:T(2,128)(2,1)} async-done(((bf16[4,2,49152]{2,1,0:T(2,128)(2,1)}), bf16[4,2,49152]{2,1,0:T(2,128)(2,1)}, u32[]{:S(2)}, u32[]{:S(2)}) %all-to-all-start.14) | async-done | bytes 786464 | tf_op jit(solution)/shard_map/all_to_all | solution.py:273
  1127.8 24.6 %all_to_all.172 = bf16[4,512,3,64]{1,3,2,0:T(8,128)(2,1)} all-to-all(bf16[4,512,3,64]{1,3,2,0:T(8,128)(2,1)} %get-tuple-element.1058), channel_id=1, replica_groups=mesh['dp'=8,'seq'=4] {'seq'}, dimensions={0} | all-to-all | bytes 1572864 | tf_op jit(solution)/shard_map/all_to_all | solution.py:263
  1160.3 15.5 all-to-all-done.13
  1190.4 10.3 convolution_add_fusion.24
  1239.7 38.0 %all-reduce.20 = (f32[768]{0:T(1024)S(1)}, f32[768]{0:T(1024)S(1)}, f32[768]{0:T(1024)S(1)}, f32[768]{0:T(1024)S(1)}, f32[768]{0:T(1024)S(1)}, /*index=5*/f32[76...) all-reduce(f32[768]{0:T(1024)S(1)} %add.724, ...), channel_id=3, replica_groups=mesh['dp'=8,'seq'=4] {'dp','seq'}, use_global_device_ids=true, to_apply=%region_37.38.clone | all-reduce | flops 9984 | bytes 79872
  1294.8 64.7 %reduce-scatter.19.cloned.1.call-done = f32[24,768]{1,0:T(8,128)} async-done(((f32[768,768]{1,0:T(8,128)}), f32[24,768]{1,0:T(8,128)}) %reduce-scatter.19.cloned.1.call-update) | async-done | bytes 73744
  1359.5 142.0 %reduce-scatter.17.cloned.1.call-done = f32[96,768]{1,0:T(8,128)} async-done(((f32[3072,768]{1,0:T(8,128)}), f32[96,768]{1,0:T(8,128)}) %reduce-scatter.17.cloned.1.call-update) | async-done | bytes 294928 | tf_op jit(solution)/shard_map/reduce_scatter | solution.py:338
  1501.5 141.4 %reduce-scatter.15.cloned.1.call-done = f32[24,3072]{1,0:T(8,128)} async-done(((f32[768,3072]{1,0:T(8,128)}), f32[24,3072]{1,0:T(8,128)}) %reduce-scatter.15.cloned.1.call-update) | async-done | bytes 294928 | tf_op jit(solution)/shard_map/reduce_scatter | solution.py:336
  (1069 shorter events, 848.1 us)
Async XLA Ops:
  7.2 60.5 %all-gather.9.cloned.1.call-start = ((), (), s32[]{:S(2)}) async-start(), calls=%async_computation.23 | async-start | bytes 1216512 | tf_op jit(solution)/shard_map/all_gather | solution.py:123
  7.9 119.6 %all-gather.7.cloned.1.call-start = ((), (), s32[]{:S(2)}) async-start(), calls=%async_computation.22 | async-start | bytes 1216512 | tf_op jit(solution)/shard_map/all_gather | solution.py:121
  8.7 178.8 %all-gather.11.cloned.1.call-start = ((), (), s32[]{:S(2)}) async-start(), calls=%async_computation.24 | async-start | bytes 1216512 | tf_op jit(solution)/shard_map/all_gather | solution.py:119
  9.4 522.3 %all-gather.13.cloned.1.call-start = ((), (), s32[]{:S(2)}) async-start(), calls=%async_computation.25 | async-start | bytes 1216512 | tf_op jit(solution)/shard_map/all_gather | solution.py:125
  10.0 528.4 %all-gather.15.cloned.1.call-start = ((), (), s32[]{:S(2)}) async-start(), calls=%async_computation.26 | async-start | bytes 4866048 | tf_op jit(solution)/shard_map/all_gather | solution.py:129
  70.9 59.6 %all-to-all-start.5 = ((bf16[512,12,64]{0,2,1:T(8,128)(2,1)}), bf16[512,12,64]{0,2,1:T(8,128)(2,1)S(1)}, u32[]{:S(2)}, u32[]{:S(2)}) async-start(bf16[512,12,64]{0,2,1:T(8,128)(2,1)} %bitcast.37), calls=%async_computation.5 | async-start | bytes 1572864 | tf_op jit(solution)/shard_map/all_to_all | solution.py:182
  130.5 60.0 %all-to-all-start.4 = ((bf16[512,12,64]{0,2,1:T(8,128)(2,1)}), bf16[512,12,64]{0,2,1:T(8,128)(2,1)}, u32[]{:S(2)}, u32[]{:S(2)}) async-start(bf16[512,12,64]{0,2,1:T(8,128)(2,1)} %bitcast.32), calls=%async_computation.4 | async-start | bytes 1572864 | tf_op jit(solution)/shard_map/all_to_all | solution.py:175
  190.5 26.0 %all-to-all-start.6 = ((bf16[512,12,64]{0,2,1:T(8,128)(2,1)}), bf16[512,12,64]{0,2,1:T(8,128)(2,1)}, u32[]{:S(2)}, u32[]{:S(2)}) async-start(bf16[512,12,64]{0,2,1:T(8,128)(2,1)} %bitcast.1115), calls=%async_computation.6 | async-start | bytes 1572864 | tf_op jit(solution)/shard_map/all_to_all | solution.py:168
  216.5 24.4 %all-to-all-start.1 = ((bf16[512,12,64]{0,2,1:T(8,128)(2,1)}), bf16[512,12,64]{0,2,1:T(8,128)(2,1)S(1)}, u32[]{:S(2)}, u32[]{:S(2)}) async-start(bf16[512,12,64]{0,2,1:T(8,128)(2,1)} %bitcast.1114), calls=%async_computation.1 | async-start | bytes 1572864 | tf_op jit(solution)/shard_map/all_to_all | solution.py:182
  220.0 325.4 %all-gather.17.cloned.1.call-start = ((), (), s32[]{:S(2)}) async-start(), calls=%async_computation.27 | async-start | bytes 4866048 | tf_op jit(solution)/shard_map/all_gather | solution.py:131
  240.9 25.1 %all-to-all-start = ((bf16[512,12,64]{0,2,1:T(8,128)(2,1)}), bf16[512,12,64]{0,2,1:T(8,128)(2,1)S(1)}, u32[]{:S(2)}, u32[]{:S(2)}) async-start(bf16[512,12,64]{0,2,1:T(8,128)(2,1)} %bitcast.1113), calls=%async_computation | async-start | bytes 1572864 | tf_op jit(solution)/shard_map/all_to_all | solution.py:175
  266.0 126.0 %all-to-all-start.2 = ((bf16[512,12,64]{0,2,1:T(8,128)(2,1)}), bf16[512,12,64]{0,2,1:T(8,128)(2,1)}, u32[]{:S(2)}, u32[]{:S(2)}) async-start(bf16[512,12,64]{0,2,1:T(8,128)(2,1)} %bitcast.14), calls=%async_computation.2 | async-start | bytes 1572864 | tf_op jit(solution)/shard_map/all_to_all | solution.py:168
  392.0 109.0 %all-to-all-start.7 = ((bf16[4,2,49152]{2,1,0:T(2,128)(2,1)}), bf16[4,2,49152]{2,1,0:T(2,128)(2,1)}, u32[]{:S(2)}, u32[]{:S(2)}) async-start(bf16[4,2,49152]{2,1,0:T(2,128)(2,1)} %reshape.1181), calls=%async_computation.7 | async-start | bytes 1572864 | tf_op jit(solution)/shard_map/all_to_all | solution.py:199
  501.0 24.2 %all-to-all-start.3 = ((bf16[4,2,49152]{2,1,0:T(2,128)(2,1)}), bf16[4,2,49152]{2,1,0:T(2,128)(2,1)S(1)}, u32[]{:S(2)}, u32[]{:S(2)}) async-start(bf16[4,2,49152]{2,1,0:T(2,128)(2,1)} %reshape.1183), calls=%async_computation.3 | async-start | bytes 1572864 | tf_op jit(solution)/shard_map/all_to_all | solution.py:199
  608.7 686.1 %reduce-scatter.13.cloned.1.call-start = ((), (), s32[]{:S(2)}) async-start(), calls=%async_computation.28 | async-start | bytes 2433024 | tf_op jit(solution)/shard_map/reduce_scatter | solution.py:332
  628.3 187.0 %all-to-all-start.12 = ((bf16[512,12,64]{0,2,1:T(8,128)(2,1)}), bf16[512,12,64]{0,2,1:T(8,128)(2,1)}, u32[]{:S(2)}, u32[]{:S(2)}) async-start(bf16[512,12,64]{0,2,1:T(8,128)(2,1)} %bitcast.101), calls=%async_computation.12 | async-start | bytes 1572864 | tf_op jit(solution)/shard_map/all_to_all | solution.py:253
  815.2 198.1 %all-to-all-start.11 = ((bf16[4,2,49152]{2,1,0:T(2,128)(2,1)}), bf16[4,2,49152]{2,1,0:T(2,128)(2,1)}, u32[]{:S(2)}, u32[]{:S(2)}) async-start(bf16[4,2,49152]{2,1,0:T(2,128)(2,1)} %reshape.1191), calls=%async_computation.11 | async-start | bytes 1572864 | tf_op jit(solution)/shard_map/all_to_all | solution.py:276
  1018.4 276.4 %reduce-scatter.23.cloned.1.call-start = ((), (), s32[]{:S(2)}) async-start(), calls=%async_computation.33 | async-start | bytes 2433024
  1058.2 23.9 %all-to-all-start.10 = ((bf16[4,2,49152]{2,1,0:T(2,128)(2,1)}), bf16[4,2,49152]{2,1,0:T(2,128)(2,1)}, u32[]{:S(2)}, u32[]{:S(2)}) async-start(bf16[4,2,49152]{2,1,0:T(2,128)(2,1)} %reshape.1189), calls=%async_computation.10 | async-start | bytes 1572864 | tf_op jit(solution)/shard_map/all_to_all | solution.py:273
  1082.1 29.8 %all-to-all-start.14 = ((bf16[4,2,49152]{2,1,0:T(2,128)(2,1)}), bf16[4,2,49152]{2,1,0:T(2,128)(2,1)}, u32[]{:S(2)}, u32[]{:S(2)}) async-start(bf16[4,2,49152]{2,1,0:T(2,128)(2,1)} %reshape.1185), calls=%async_computation.14 | async-start | bytes 1572864 | tf_op jit(solution)/shard_map/all_to_all | solution.py:273
  1086.3 208.5 %reduce-scatter.21.cloned.1.call-start = ((), (), s32[]{:S(2)}) async-start(), calls=%async_computation.32 | async-start | bytes 2433024
  1156.6 202.9 %reduce-scatter.19.cloned.1.call-start = ((), (), s32[]{:S(2)}) async-start(), calls=%async_computation.31 | async-start | bytes 2433024
  1183.3 318.2 %reduce-scatter.17.cloned.1.call-start = ((), (), s32[]{:S(2)}) async-start(), calls=%async_computation.30 | async-start | bytes 9732096 | tf_op jit(solution)/shard_map/reduce_scatter | solution.py:338
  1200.8 442.2 %reduce-scatter.15.cloned.1.call-start = ((), (), s32[]{:S(2)}) async-start(), calls=%async_computation.29 | async-start | bytes 9732096 | tf_op jit(solution)/shard_map/reduce_scatter | solution.py:336
  (174 other events, 1333.9 us)
Sparse Core Ops, SparseCore 0:
  10.8 56.8 all-gather.8
  70.5 56.9 all-gather.6
  130.3 57.1 all-gather.10
  190.2 65.8 all-gather.12
  258.7 71.9 all-gather.14
  333.3 61.8 all-gather.16
  615.3 100.2 reduce-scatter.12
  1050.0 100.7 reduce-scatter.22
  1156.7 98.4 reduce-scatter.20
  1260.9 98.5 reduce-scatter.18
  1366.0 135.4 reduce-scatter.16
  1507.9 135.0 reduce-scatter.14
